TPU v7x, 128 devices: a whole 4x4x4 slice. The times are simulated.
128 devices in a mesh: row: 8 (over z, x_hi), col: 16 (over x_lo, y, core).
Axes of the slice: x: 4 (x_hi: 2, x_lo: 2; x = x_hi * 2 + x_lo), y: 4, z: 4, core: 2. Of those that a mesh axis runs over, the one named last changes fastest.
Arguments:
- embeddings: bfloat16 [32768, 768], P(('row', 'col'))
- spread: bfloat16 [32768], P(('row', 'col')), may hold values from 1 to 16
- features: bfloat16 [32768, 256], P(('row', 'col')), may hold values from -160 to 160
- block_list: int32 [256], replicated, may hold values from 0 to 63
- list_pairs: int32 [64, 64], replicated, may hold values from 0 to 1, as said below
Outputs:
- smoothed: float32 [32768, 256], P(('row', 'col'))
Inputs may be any that keep to these rules, and one draw needn't show every extreme that they name: `list_pairs`: symmetric, with ones on the diagonal.
All inputs are finite; a program needn't handle non-finite values.
Results may differ from a plain program's by a relative error of at most 0.0029.
Values may be sent and summed in bfloat16 or wider, within the bound.
A program may use at most 64 MiB of HBM per device.

v0:
```python
import math
import jax
import jax.numpy as jnp
from jax import lax
from jax.sharding import PartitionSpec as P

BLK = 128
LISTS = 64


def active_table(block_list, list_pairs, row_blocks, col_blocks):
    count = block_list.shape[0]
    lists_onehot = (block_list[:, None] == jnp.arange(LISTS, dtype=jnp.int32)[None, :]).astype(
        jnp.float32
    )
    pair_table = list_pairs.astype(jnp.float32)
    row_select = (row_blocks[:, None] == jnp.arange(count, dtype=jnp.int32)[None, :]).astype(
        jnp.float32
    )
    col_select = (col_blocks[:, None] == jnp.arange(count, dtype=jnp.int32)[None, :]).astype(
        jnp.float32
    )
    row_onehot = jnp.dot(row_select, lists_onehot, precision=lax.Precision.HIGHEST)
    col_onehot = jnp.dot(col_select, lists_onehot, precision=lax.Precision.HIGHEST)
    joined = jnp.dot(row_onehot, pair_table, precision=lax.Precision.HIGHEST)
    return jnp.dot(joined, col_onehot.T, precision=lax.Precision.HIGHEST)


def shards(embeddings, spread, features, block_list, list_pairs):
    rows_x, rows_beta = (
        lax.all_gather(embeddings, "col", axis=0, tiled=True),
        lax.all_gather(spread, "col", axis=0, tiled=True),
    )
    cols_x, cols_beta, cols_feat = (
        lax.all_gather(embeddings, "row", axis=0, tiled=True),
        lax.all_gather(spread, "row", axis=0, tiled=True),
        lax.all_gather(features, "row", axis=0, tiled=True),
    )
    own_count = embeddings.shape[0]
    col_size = lax.axis_size("col")
    row_index = lax.axis_index("row")
    col_index = lax.axis_index("col")
    total_rows = rows_x.shape[0]
    total_cols = cols_x.shape[0]
    row_ids = row_index * total_rows + jnp.arange(total_rows, dtype=jnp.int32)
    local_index = jnp.arange(total_cols, dtype=jnp.int32)
    col_ids = (
        local_index // own_count * col_size + col_index
    ) * own_count + local_index % own_count
    active = active_table(block_list, list_pairs, row_ids[::BLK] // BLK, col_ids[::BLK] // BLK)
    col_blocks = active.shape[1]
    row_norm = jnp.sum(jnp.square(rows_x.astype(jnp.float32)), axis=1)
    col_norm = jnp.sum(jnp.square(cols_x.astype(jnp.float32)), axis=1)
    row_bw = rows_beta.astype(jnp.float32)
    col_bw = cols_beta.astype(jnp.float32)

    def block_terms(start, size):
        row_emb = lax.dynamic_slice_in_dim(rows_x, start, size, 0)
        norm_part = lax.dynamic_slice_in_dim(row_norm, start, size, 0)
        beta_part = lax.dynamic_slice_in_dim(row_bw, start, size, 0)
        ids_part = lax.dynamic_slice_in_dim(row_ids, start, size, 0)
        inner = lax.dot_general(
            row_emb, cols_x, (((1,), (1,)), ((), ())), preferred_element_type=jnp.float32
        )
        dist = norm_part[:, None] + col_norm[None, :] - 2.0 * inner
        active_part = lax.dynamic_slice_in_dim(active, start // BLK, size // BLK, 0)
        expanded = jnp.broadcast_to(
            active_part[:, None, :, None], (size // BLK, BLK, col_blocks, BLK)
        )
        mask = expanded.reshape(size, total_cols) * (ids_part[:, None] != col_ids[None, :]).astype(
            jnp.float32
        )
        near = mask * jnp.exp(-beta_part[:, None] * dist)
        return (mask, dist, near)

    block_rows = math.gcd(total_rows, 512)
    starts = jnp.arange(total_rows // block_rows, dtype=jnp.int32) * block_rows
    row_partial = lax.map(
        lambda start: jnp.sum(block_terms(start, block_rows)[2], axis=1), starts
    ).reshape(total_rows)
    row_totals = lax.psum(row_partial, "col")
    own_totals = lax.dynamic_slice_in_dim(row_totals, col_index * own_count, own_count, 0)
    col_totals = lax.all_gather(own_totals, "row", axis=0, tiled=True)
    size = math.gcd(total_rows, 512)

    def one_block(begin):
        mask, dist, near = block_terms(begin, size)
        far = mask * jnp.exp(-col_bw[None, :] * dist)
        total_part = lax.dynamic_slice_in_dim(row_totals, begin, size, 0)
        weight = ((near / total_part[:, None] + far / col_totals[None, :]) * 0.5).astype(
            jnp.bfloat16
        )
        return jnp.dot(weight, cols_feat, preferred_element_type=jnp.float32)

    begins = 0 + jnp.arange(total_rows // size, dtype=jnp.int32) * size
    partial_out = lax.map(one_block, begins).reshape(total_rows, cols_feat.shape[1])
    summed = lax.psum(partial_out, "col")
    return lax.dynamic_slice_in_dim(summed, col_index * own_count, own_count, 0)


def solution(mesh):
    return jax.shard_map(
        shards,
        mesh=mesh,
        in_specs=(P(("row", "col"), None), P(("row", "col")), P(("row", "col"), None), P(), P()),
        out_specs=P(("row", "col"), None),
        check_vma=False,
    )
```

profile of v0, /device:TPU:1, one launch (start us, length us, event | category | flops | bytes accessed | tf_op | source)
XLA Modules:
  0.0 548.1 jit_solution(9659464464459559050)
XLA Ops:
  6.5 0.7 all-gather.9.cloned.1.call-update
  7.3 0.7 all-gather.7.cloned.1.call-update
  8.1 0.7 all-gather.11.cloned.1.call-update
  8.8 0.7 reshape.44
  9.5 21.2 %all-gather = bf16[16,1,256]{2,1,0:T(2,128)(2,1)S(1)} all-gather(bf16[1,1,256]{2,1,0:T(2,128)(2,1)S(1)} %reshape.44), channel_id=1, replica_groups=mesh['row'=8,'col'=16] {'col'}, dimensions={0}, use_global_device_ids=true | all-gather | bytes 8704 | tf_op jit(solution)/shard_map/all_gather | solution.py:32
  30.6 20.6 %all-gather.1 = bf16[8,1,256]{2,1,0:T(2,128)(2,1)S(1)} all-gather(bf16[1,1,256]{2,1,0:T(2,128)(2,1)S(1)} %reshape.44), channel_id=1, replica_groups=mesh['row'=8,'col'=16] {'row'}, dimensions={0}, use_global_device_ids=true | all-gather | bytes 4608 | tf_op jit(solution)/shard_map/all_gather | solution.py:36
  51.5 0.9 fusion.40
  52.4 0.9 fusion.41
  53.3 0.9 fusion.44
  54.4 21.0 %all-gather.9.cloned.1.call-done = bf16[2048,768]{1,0:T(8,128)(2,1)} async-done(((bf16[256,768]{1,0:T(8,128)(2,1)}), bf16[2048,768]{1,0:T(8,128)(2,1)}) %all-gather.9.cloned.1.call-update) | async-done | bytes 3145744 | tf_op jit(solution)/shard_map/all_gather | solution.py:35
  75.3 2.7 multiply_reduce_fusion.1
  78.1 39.8 %all-gather.7.cloned.1.call-done = bf16[4096,768]{1,0:T(8,128)(2,1)} async-done(((bf16[256,768]{1,0:T(8,128)(2,1)}), bf16[4096,768]{1,0:T(8,128)(2,1)}) %all-gather.7.cloned.1.call-update) | async-done | bytes 6291472 | tf_op jit(solution)/shard_map/all_gather | solution.py:31
  117.9 4.1 multiply_reduce_fusion
  122.0 102.0 %while.26 = (s32[]{:T(128)}, f32[8,512]{1,0:T(8,128)S(1)}, s32[8]{0:T(128)S(1)}, s32[4096]{0:T(1024)S(1)}, f32[32,16]{1,0:T(8,128)S(1)}, /*index=5*/f32[4096]{0:...) while((s32[]{:T(128)}, f32[8,512]{1,0:T(8,128)S(1)}, ...), condition=%wide.region_4.5_spmd.clone, body=%wide.region_2.4_spmd.clone.sunk | while | flops 1619034112 | bytes 12371102 | solution.py:78
  122.0 0.6 dynamic_slice.126
  125.1 2.4 broadcast_in_dim.65
  129.0 5.8 %fusion.78 = f32[512]{0:T(512)S(1)} fusion(f32[64,8,16,128]{3,2,1,0:T(8,128)} %bitcast.66, bf16[2048,768]{1,0:T(8,128)(2,1)S(1)} %get-tuple-element.698, f32[2048]{0:T(1024)S(1)} %get-tuple-element.696, f32[512]{0:T(512)S(1)} %dynamic_slice.127, f32[512]{0:T(512)S(1)} %dynamic-slice_negate_fusion.4, s32[2048]{0:T(1024)S(1)} %fusion.77, ...), kind=kOutput, calls=%fused_computation.4.clone.1 | convolution fusion | flops 1619000832 | bytes 8151044 | tf_op jit(solution)/shard_map/while/body/eval_jaxpr/dot_general | solution.py:62
  134.8 0.6 dynamic_slice.126
  137.9 2.4 broadcast_in_dim.65
  141.8 5.7 %fusion.78 = f32[512]{0:T(512)S(1)} fusion(f32[64,8,16,128]{3,2,1,0:T(8,128)} %bitcast.66, bf16[2048,768]{1,0:T(8,128)(2,1)S(1)} %get-tuple-element.698, f32[2048]{0:T(1024)S(1)} %get-tuple-element.696, f32[512]{0:T(512)S(1)} %dynamic_slice.127, f32[512]{0:T(512)S(1)} %dynamic-slice_negate_fusion.4, s32[2048]{0:T(1024)S(1)} %fusion.77, ...), kind=kOutput, calls=%fused_computation.4.clone.1 | convolution fusion | flops 1619000832 | bytes 8151044 | tf_op jit(solution)/shard_map/while/body/eval_jaxpr/dot_general | solution.py:62
  147.6 0.6 dynamic_slice.126
  150.7 2.4 broadcast_in_dim.65
  154.6 5.7 %fusion.78 = f32[512]{0:T(512)S(1)} fusion(f32[64,8,16,128]{3,2,1,0:T(8,128)} %bitcast.66, bf16[2048,768]{1,0:T(8,128)(2,1)S(1)} %get-tuple-element.698, f32[2048]{0:T(1024)S(1)} %get-tuple-element.696, f32[512]{0:T(512)S(1)} %dynamic_slice.127, f32[512]{0:T(512)S(1)} %dynamic-slice_negate_fusion.4, s32[2048]{0:T(1024)S(1)} %fusion.77, ...), kind=kOutput, calls=%fused_computation.4.clone.1 | convolution fusion | flops 1619000832 | bytes 8151044 | tf_op jit(solution)/shard_map/while/body/eval_jaxpr/dot_general | solution.py:62
  160.3 0.6 dynamic_slice.126
  163.4 2.4 broadcast_in_dim.65
  167.3 5.7 %fusion.78 = f32[512]{0:T(512)S(1)} fusion(f32[64,8,16,128]{3,2,1,0:T(8,128)} %bitcast.66, bf16[2048,768]{1,0:T(8,128)(2,1)S(1)} %get-tuple-element.698, f32[2048]{0:T(1024)S(1)} %get-tuple-element.696, f32[512]{0:T(512)S(1)} %dynamic_slice.127, f32[512]{0:T(512)S(1)} %dynamic-slice_negate_fusion.4, s32[2048]{0:T(1024)S(1)} %fusion.77, ...), kind=kOutput, calls=%fused_computation.4.clone.1 | convolution fusion | flops 1619000832 | bytes 8151044 | tf_op jit(solution)/shard_map/while/body/eval_jaxpr/dot_general | solution.py:62
  173.1 0.6 dynamic_slice.126
  176.2 2.4 broadcast_in_dim.65
  180.1 5.7 %fusion.78 = f32[512]{0:T(512)S(1)} fusion(f32[64,8,16,128]{3,2,1,0:T(8,128)} %bitcast.66, bf16[2048,768]{1,0:T(8,128)(2,1)S(1)} %get-tuple-element.698, f32[2048]{0:T(1024)S(1)} %get-tuple-element.696, f32[512]{0:T(512)S(1)} %dynamic_slice.127, f32[512]{0:T(512)S(1)} %dynamic-slice_negate_fusion.4, s32[2048]{0:T(1024)S(1)} %fusion.77, ...), kind=kOutput, calls=%fused_computation.4.clone.1 | convolution fusion | flops 1619000832 | bytes 8151044 | tf_op jit(solution)/shard_map/while/body/eval_jaxpr/dot_general | solution.py:62
  185.8 0.6 dynamic_slice.126
  188.9 2.4 broadcast_in_dim.65
  192.8 5.7 %fusion.78 = f32[512]{0:T(512)S(1)} fusion(f32[64,8,16,128]{3,2,1,0:T(8,128)} %bitcast.66, bf16[2048,768]{1,0:T(8,128)(2,1)S(1)} %get-tuple-element.698, f32[2048]{0:T(1024)S(1)} %get-tuple-element.696, f32[512]{0:T(512)S(1)} %dynamic_slice.127, f32[512]{0:T(512)S(1)} %dynamic-slice_negate_fusion.4, s32[2048]{0:T(1024)S(1)} %fusion.77, ...), kind=kOutput, calls=%fused_computation.4.clone.1 | convolution fusion | flops 1619000832 | bytes 8151044 | tf_op jit(solution)/shard_map/while/body/eval_jaxpr/dot_general | solution.py:62
  198.5 0.6 dynamic_slice.126
  201.6 2.4 broadcast_in_dim.65
  205.5 5.7 %fusion.78 = f32[512]{0:T(512)S(1)} fusion(f32[64,8,16,128]{3,2,1,0:T(8,128)} %bitcast.66, bf16[2048,768]{1,0:T(8,128)(2,1)S(1)} %get-tuple-element.698, f32[2048]{0:T(1024)S(1)} %get-tuple-element.696, f32[512]{0:T(512)S(1)} %dynamic_slice.127, f32[512]{0:T(512)S(1)} %dynamic-slice_negate_fusion.4, s32[2048]{0:T(1024)S(1)} %fusion.77, ...), kind=kOutput, calls=%fused_computation.4.clone.1 | convolution fusion | flops 1619000832 | bytes 8151044 | tf_op jit(solution)/shard_map/while/body/eval_jaxpr/dot_general | solution.py:62
  211.3 0.6 dynamic_slice.126
  214.4 2.4 broadcast_in_dim.65
  218.3 5.7 %fusion.78 = f32[512]{0:T(512)S(1)} fusion(f32[64,8,16,128]{3,2,1,0:T(8,128)} %bitcast.66, bf16[2048,768]{1,0:T(8,128)(2,1)S(1)} %get-tuple-element.698, f32[2048]{0:T(1024)S(1)} %get-tuple-element.696, f32[512]{0:T(512)S(1)} %dynamic_slice.127, f32[512]{0:T(512)S(1)} %dynamic-slice_negate_fusion.4, s32[2048]{0:T(1024)S(1)} %fusion.77, ...), kind=kOutput, calls=%fused_computation.4.clone.1 | convolution fusion | flops 1619000832 | bytes 8151044 | tf_op jit(solution)/shard_map/while/body/eval_jaxpr/dot_general | solution.py:62
  224.0 51.3 %psum.14 = f32[4096]{0:T(1024)S(1)} all-reduce(f32[4096]{0:T(1024)S(1)} %bitcast.69), channel_id=1, replica_groups=mesh['row'=8,'col'=16] {'col'}, use_global_device_ids=true, to_apply=%region_5.6 | all-reduce | flops 4096 | bytes 32768 | tf_op jit(solution)/shard_map/psum | solution.py:81
  275.4 19.4 %all-gather.2 = f32[8,1,256]{2,1,0:T(1,128)S(1)} all-gather(f32[1,1,256]{2,1,0:T(1,128)S(1)} %bitcast.75), channel_id=1, replica_groups=mesh['row'=8,'col'=16] {'row'}, dimensions={0}, use_global_device_ids=true | all-gather | bytes 9216 | tf_op jit(solution)/shard_map/all_gather | solution.py:83
  294.8 114.9 %while.27 = (s32[]{:T(128)}, f32[8,512,256]{2,1,0:T(8,128)}, s32[8]{0:T(128)S(1)}, s32[4096]{0:T(1024)S(1)}, f32[32,16]{1,0:T(8,128)S(1)}, /*index=5*/f32[4096]{...) while((s32[]{:T(128)}, f32[8,512,256]{2,1,0:T(8,128)}, ...), condition=%wide.region_7.8_spmd.clone, body=%wide.region_6.7_spmd.clone.sunk | while | flops 2162196992 | bytes 13960894 | solution.py:96
  294.8 0.6 dynamic_slice.132
  297.7 2.4 broadcast_in_dim.66
  301.6 7.6 %fusion.83 = f32[8,512,256]{2,1,0:T(8,128)} fusion(f32[8,512,256]{2,1,0:T(8,128)} %get-tuple-element.730, s32[]{:T(128)} %get-tuple-element.729, bf16[2048,256]{1,0:T(8,128)(2,1)} %get-tuple-element.764, f32[64,8,16,128]{3,2,1,0:T(8,128)} %bitcast.65, bf16[2048,768]{1,0:T(8,128)(2,1)S(1)} %get-tuple-element.760, f32[2048]{0:T(1024)S(1)} %get-tuple-element.763, ...), kind=kOutput, calls=%fused_computation.28.clone.1 | convolution fusion | flops 2162163712 | bytes 9740804 | tf_op jit(solution)/shard_map/while/body/eval_jaxpr/dot_general | solution.py:93
  309.2 0.6 dynamic_slice.132
  312.0 2.4 broadcast_in_dim.66
  315.9 7.6 %fusion.83 = f32[8,512,256]{2,1,0:T(8,128)} fusion(f32[8,512,256]{2,1,0:T(8,128)} %get-tuple-element.730, s32[]{:T(128)} %get-tuple-element.729, bf16[2048,256]{1,0:T(8,128)(2,1)} %get-tuple-element.764, f32[64,8,16,128]{3,2,1,0:T(8,128)} %bitcast.65, bf16[2048,768]{1,0:T(8,128)(2,1)S(1)} %get-tuple-element.760, f32[2048]{0:T(1024)S(1)} %get-tuple-element.763, ...), kind=kOutput, calls=%fused_computation.28.clone.1 | convolution fusion | flops 2162163712 | bytes 9740804 | tf_op jit(solution)/shard_map/while/body/eval_jaxpr/dot_general | solution.py:93
  323.5 0.6 dynamic_slice.132
  326.4 2.4 broadcast_in_dim.66
  330.3 7.6 %fusion.83 = f32[8,512,256]{2,1,0:T(8,128)} fusion(f32[8,512,256]{2,1,0:T(8,128)} %get-tuple-element.730, s32[]{:T(128)} %get-tuple-element.729, bf16[2048,256]{1,0:T(8,128)(2,1)} %get-tuple-element.764, f32[64,8,16,128]{3,2,1,0:T(8,128)} %bitcast.65, bf16[2048,768]{1,0:T(8,128)(2,1)S(1)} %get-tuple-element.760, f32[2048]{0:T(1024)S(1)} %get-tuple-element.763, ...), kind=kOutput, calls=%fused_computation.28.clone.1 | convolution fusion | flops 2162163712 | bytes 9740804 | tf_op jit(solution)/shard_map/while/body/eval_jaxpr/dot_general | solution.py:93
  337.9 0.6 dynamic_slice.132
  340.7 2.4 broadcast_in_dim.66
  344.6 7.6 %fusion.83 = f32[8,512,256]{2,1,0:T(8,128)} fusion(f32[8,512,256]{2,1,0:T(8,128)} %get-tuple-element.730, s32[]{:T(128)} %get-tuple-element.729, bf16[2048,256]{1,0:T(8,128)(2,1)} %get-tuple-element.764, f32[64,8,16,128]{3,2,1,0:T(8,128)} %bitcast.65, bf16[2048,768]{1,0:T(8,128)(2,1)S(1)} %get-tuple-element.760, f32[2048]{0:T(1024)S(1)} %get-tuple-element.763, ...), kind=kOutput, calls=%fused_computation.28.clone.1 | convolution fusion | flops 2162163712 | bytes 9740804 | tf_op jit(solution)/shard_map/while/body/eval_jaxpr/dot_general | solution.py:93
  352.2 0.6 dynamic_slice.132
  355.1 2.4 broadcast_in_dim.66
  359.0 7.6 %fusion.83 = f32[8,512,256]{2,1,0:T(8,128)} fusion(f32[8,512,256]{2,1,0:T(8,128)} %get-tuple-element.730, s32[]{:T(128)} %get-tuple-element.729, bf16[2048,256]{1,0:T(8,128)(2,1)} %get-tuple-element.764, f32[64,8,16,128]{3,2,1,0:T(8,128)} %bitcast.65, bf16[2048,768]{1,0:T(8,128)(2,1)S(1)} %get-tuple-element.760, f32[2048]{0:T(1024)S(1)} %get-tuple-element.763, ...), kind=kOutput, calls=%fused_computation.28.clone.1 | convolution fusion | flops 2162163712 | bytes 9740804 | tf_op jit(solution)/shard_map/while/body/eval_jaxpr/dot_general | solution.py:93
  369.5 2.4 broadcast_in_dim.66
  373.4 7.7 %fusion.83 = f32[8,512,256]{2,1,0:T(8,128)} fusion(f32[8,512,256]{2,1,0:T(8,128)} %get-tuple-element.730, s32[]{:T(128)} %get-tuple-element.729, bf16[2048,256]{1,0:T(8,128)(2,1)} %get-tuple-element.764, f32[64,8,16,128]{3,2,1,0:T(8,128)} %bitcast.65, bf16[2048,768]{1,0:T(8,128)(2,1)S(1)} %get-tuple-element.760, f32[2048]{0:T(1024)S(1)} %get-tuple-element.763, ...), kind=kOutput, calls=%fused_computation.28.clone.1 | convolution fusion | flops 2162163712 | bytes 9740804 | tf_op jit(solution)/shard_map/while/body/eval_jaxpr/dot_general | solution.py:93
  383.9 2.4 broadcast_in_dim.66
  387.8 7.6 %fusion.83 = f32[8,512,256]{2,1,0:T(8,128)} fusion(f32[8,512,256]{2,1,0:T(8,128)} %get-tuple-element.730, s32[]{:T(128)} %get-tuple-element.729, bf16[2048,256]{1,0:T(8,128)(2,1)} %get-tuple-element.764, f32[64,8,16,128]{3,2,1,0:T(8,128)} %bitcast.65, bf16[2048,768]{1,0:T(8,128)(2,1)S(1)} %get-tuple-element.760, f32[2048]{0:T(1024)S(1)} %get-tuple-element.763, ...), kind=kOutput, calls=%fused_computation.28.clone.1 | convolution fusion | flops 2162163712 | bytes 9740804 | tf_op jit(solution)/shard_map/while/body/eval_jaxpr/dot_general | solution.py:93
  398.2 2.4 broadcast_in_dim.66
  402.1 7.6 %fusion.83 = f32[8,512,256]{2,1,0:T(8,128)} fusion(f32[8,512,256]{2,1,0:T(8,128)} %get-tuple-element.730, s32[]{:T(128)} %get-tuple-element.729, bf16[2048,256]{1,0:T(8,128)(2,1)} %get-tuple-element.764, f32[64,8,16,128]{3,2,1,0:T(8,128)} %bitcast.65, bf16[2048,768]{1,0:T(8,128)(2,1)S(1)} %get-tuple-element.760, f32[2048]{0:T(1024)S(1)} %get-tuple-element.763, ...), kind=kOutput, calls=%fused_computation.28.clone.1 | convolution fusion | flops 2162163712 | bytes 9740804 | tf_op jit(solution)/shard_map/while/body/eval_jaxpr/dot_general | solution.py:93
  409.7 130.2 %all-reduce.2.cloned.1.call-done = f32[4096,256]{1,0:T(8,128)} async-done(((f32[4096,256]{1,0:T(8,128)}), f32[4096,256]{1,0:T(8,128)}) %all-reduce.2.cloned.1.call-update) | async-done | bytes 4194320 | tf_op jit(solution)/shard_map/psum | solution.py:97
  539.9 1.7 constant_dynamic-slice_fusion.2
  (121 shorter events, 7.4 us)
Async XLA Ops:
  6.5 68.8 %all-gather.9.cloned.1.call-start = ((), (), s32[]{:S(2)}) async-start(), calls=%async_computation.1 | async-start | bytes 3538944 | tf_op jit(solution)/shard_map/all_gather | solution.py:35
  7.3 110.6 %all-gather.7.cloned.1.call-start = ((), (), s32[]{:S(2)}) async-start(), calls=%async_computation | async-start | bytes 6684672 | tf_op jit(solution)/shard_map/all_gather | solution.py:31
  8.0 286.8 %all-gather.11.cloned.1.call-start = ((), (), s32[]{:S(2)}) async-start(), calls=%async_computation.2 | async-start | bytes 1179648 | tf_op jit(solution)/shard_map/all_gather | solution.py:37
  8.7 531.2 %all-reduce.2.cloned.1.call-start = ((), (), s32[]{:S(2)}) async-start(), calls=%async_computation.3 | async-start | bytes 8388608 | tf_op jit(solution)/shard_map/psum | solution.py:97
  75.3 46.6 %copy-start = (bf16[2048,768]{1,0:T(8,128)(2,1)S(1)}, bf16[2048,768]{1,0:T(8,128)(2,1)}, u32[]{:S(2)}) copy-start(bf16[2048,768]{1,0:T(8,128)(2,1)} %all-gather.9.cloned.1.call-done) | copy-start | bytes 9437188
Sparse Core Ops, SparseCore 0:
  9.7 65.6 all-gather.8
  77.0 40.7 all-gather.6
  120.2 45.7 all-gather.10
  409.9 130.0 all-reduce.1
where the time goes:
time: 549 us; the launch traced here: 548 us
  waiting for transfers between devices  193 us (35%)
  blocking collectives  112 us (20%)
  matrix products  109 us (20%)
  loops' own time  57.7 us (11%)
  local copies, waits for them, and re-layouts  54 us (10%)
  between operations  13.2 us (2%)
  other arithmetic  8.3 us (2%)
    psum x1, waiting for transfers between devices, shards(): summed = lax.psum(partial_out, 'col')  130 us
    dot_general x8, matrix products, one_block(): return jnp.dot(weight, cols_feat, preferred_element_type=jnp.float32)  61 us
    psum x1, blocking collectives, shards(): row_totals = lax.psum(row_partial, 'col')  51.3 us
    dot_general x8, matrix products, block_terms(): lax.dot_general(row_emb, cols_x, (((1,), (1,)), ((), ())), preferred_elem...  45.4 us
    all_gather x1, waiting for transfers between devices, shards(): lax.all_gather(embeddings, 'col', axis=0, tiled=True)  39.8 us
    broadcast_in_dim x16, local copies, waits for them, and re-layouts, block_terms(): jnp.broadcast_to(active_part[:, None, :, None], (size // BLK, BLK, col_bl...  38.6 us
    another operation x1, loops' own time, shards(): lax.map(lambda start: jnp.sum(block_terms(start, block_rows)[2], axis=1),...  30.1 us
    another operation x1, loops' own time, shards(): lax.map(one_block, begins).reshape(total_rows, cols_feat.shape[1])  27.6 us
  transfers between devices with their start and end apart: 4, of which 3 were waited for; matrix products, arithmetic and copies ran while one was open for 15% of the time, Pallas kernels for 0%

commit v1 on v0

--- a/solution.py
+++ b/solution.py
@@ -78,7 +78,7 @@
     row_partial = lax.map(
         lambda start: jnp.sum(block_terms(start, block_rows)[2], axis=1), starts
     ).reshape(total_rows)
-    row_totals = lax.psum(row_partial, "col")
+    row_totals = jnp.sum(lax.all_gather(row_partial, "col"), axis=0)
     own_totals = lax.dynamic_slice_in_dim(row_totals, col_index * own_count, own_count, 0)
     col_totals = lax.all_gather(own_totals, "row", axis=0, tiled=True)
     size = math.gcd(total_rows, 512)

time: 549 us -> 513 us (0.934)
  blocking collectives: 112 us -> 80.8 us
    psum x1 -> x0, blocking collectives: 51.3 us -> none  [shards(): row_totals = lax.psum(row_partial, 'col')]
    all_gather x0 -> x1, blocking collectives: none -> 19.6 us  [shards(): row_totals = jnp.sum(lax.all_gather(row_partial, 'col'), axis=0)]
  transfers between devices with their start and end apart: 4 -> 4, of which waited for: 3 -> 3; matrix products, arithmetic and copies ran while one was open for 15% -> 16% of each run, Pallas kernels for 0% -> 0%
where the time goes in v1:
time: 513 us; the launch traced here: 512 us
  waiting for transfers between devices  189 us (37%)
  matrix products  109 us (21%)
  blocking collectives  80.8 us (16%)
  loops' own time  57.7 us (11%)
  local copies, waits for them, and re-layouts  54.1 us (11%)
  between operations  13.2 us (3%)
  other arithmetic  8.47 us (2%)
    psum x1, waiting for transfers between devices, shards(): summed = lax.psum(partial_out, 'col')  126 us
    dot_general x8, matrix products, one_block(): return jnp.dot(weight, cols_feat, preferred_element_type=jnp.float32)  60.9 us
    dot_general x8, matrix products, block_terms(): lax.dot_general(row_emb, cols_x, (((1,), (1,)), ((), ())), preferred_elem...  45.2 us
    all_gather x1, waiting for transfers between devices, shards(): lax.all_gather(embeddings, 'col', axis=0, tiled=True)  39.8 us
    broadcast_in_dim x16, local copies, waits for them, and re-layouts, block_terms(): jnp.broadcast_to(active_part[:, None, :, None], (size // BLK, BLK, col_bl...  38.6 us
    another operation x1, loops' own time, shards(): lax.map(lambda start: jnp.sum(block_terms(start, block_rows)[2], axis=1),...  30.1 us
    another operation x1, loops' own time, shards(): lax.map(one_block, begins).reshape(total_rows, cols_feat.shape[1])  27.6 us
    all_gather x1, blocking collectives, shards(): lax.all_gather(spread, 'col', axis=0, tiled=True)  21.2 us
  transfers between devices with their start and end apart: 4, of which 3 were waited for; matrix products, arithmetic and copies ran while one was open for 16% of the time, Pallas kernels for 0%

profile of v1, /device:TPU:1, one launch (start us, length us, event | category | flops | bytes accessed | tf_op | source)
XLA Modules:
  0.0 512.2 jit_solution(4506874127202068376)
XLA Ops:
  6.5 0.7 all-gather.10.cloned.1.call-update
  7.3 0.7 all-gather.8.cloned.1.call-update
  8.1 0.7 all-gather.12.cloned.1.call-update
  8.8 0.7 reshape.40
  9.5 21.2 %all-gather = bf16[16,1,256]{2,1,0:T(2,128)(2,1)S(1)} all-gather(bf16[1,1,256]{2,1,0:T(2,128)(2,1)S(1)} %reshape.40), channel_id=1, replica_groups=mesh['row'=8,'col'=16] {'col'}, dimensions={0}, use_global_device_ids=true | all-gather | bytes 8704 | tf_op jit(solution)/shard_map/all_gather | solution.py:32
  30.6 20.6 %all-gather.2 = bf16[8,1,256]{2,1,0:T(2,128)(2,1)S(1)} all-gather(bf16[1,1,256]{2,1,0:T(2,128)(2,1)S(1)} %reshape.40), channel_id=1, replica_groups=mesh['row'=8,'col'=16] {'row'}, dimensions={0}, use_global_device_ids=true | all-gather | bytes 4608 | tf_op jit(solution)/shard_map/all_gather | solution.py:36
  51.5 0.9 fusion.40
  52.4 0.9 fusion.41
  53.3 0.9 fusion.44
  54.4 21.0 %all-gather.10.cloned.1.call-done = bf16[2048,768]{1,0:T(8,128)(2,1)} async-done(((bf16[256,768]{1,0:T(8,128)(2,1)}), bf16[2048,768]{1,0:T(8,128)(2,1)}) %all-gather.10.cloned.1.call-update) | async-done | bytes 3145744 | tf_op jit(solution)/shard_map/all_gather | solution.py:35
  75.3 2.7 multiply_reduce_fusion.1
  78.1 39.8 %all-gather.8.cloned.1.call-done = bf16[4096,768]{1,0:T(8,128)(2,1)} async-done(((bf16[256,768]{1,0:T(8,128)(2,1)}), bf16[4096,768]{1,0:T(8,128)(2,1)}) %all-gather.8.cloned.1.call-update) | async-done | bytes 6291472 | tf_op jit(solution)/shard_map/all_gather | solution.py:31
  117.9 4.1 multiply_reduce_fusion
  122.0 101.8 %while.26 = (s32[]{:T(128)}, f32[8,512]{1,0:T(8,128)S(1)}, s32[8]{0:T(128)S(1)}, s32[4096]{0:T(1024)S(1)}, f32[32,16]{1,0:T(8,128)S(1)}, /*index=5*/f32[4096]{0:...) while((s32[]{:T(128)}, f32[8,512]{1,0:T(8,128)S(1)}, ...), condition=%wide.region_4.5_spmd.clone, body=%wide.region_2.4_spmd.clone.sunk | while | flops 1619034112 | bytes 12371102 | solution.py:78
  122.0 0.6 dynamic_slice.126
  125.1 2.4 broadcast_in_dim.65
  129.0 5.7 %fusion.78 = f32[512]{0:T(512)S(1)} fusion(f32[64,8,16,128]{3,2,1,0:T(8,128)} %bitcast.64, bf16[2048,768]{1,0:T(8,128)(2,1)S(1)} %get-tuple-element.698, f32[2048]{0:T(1024)S(1)} %get-tuple-element.696, f32[512]{0:T(512)S(1)} %dynamic_slice.127, f32[512]{0:T(512)S(1)} %dynamic-slice_negate_fusion.4, s32[2048]{0:T(1024)S(1)} %fusion.77, ...), kind=kOutput, calls=%fused_computation.4.clone.1 | convolution fusion | flops 1619000832 | bytes 8151044 | tf_op jit(solution)/shard_map/while/body/eval_jaxpr/dot_general | solution.py:62
  134.8 0.6 dynamic_slice.126
  137.9 2.4 broadcast_in_dim.65
  141.8 5.6 %fusion.78 = f32[512]{0:T(512)S(1)} fusion(f32[64,8,16,128]{3,2,1,0:T(8,128)} %bitcast.64, bf16[2048,768]{1,0:T(8,128)(2,1)S(1)} %get-tuple-element.698, f32[2048]{0:T(1024)S(1)} %get-tuple-element.696, f32[512]{0:T(512)S(1)} %dynamic_slice.127, f32[512]{0:T(512)S(1)} %dynamic-slice_negate_fusion.4, s32[2048]{0:T(1024)S(1)} %fusion.77, ...), kind=kOutput, calls=%fused_computation.4.clone.1 | convolution fusion | flops 1619000832 | bytes 8151044 | tf_op jit(solution)/shard_map/while/body/eval_jaxpr/dot_general | solution.py:62
  147.5 0.6 dynamic_slice.126
  150.6 2.4 broadcast_in_dim.65
  154.5 5.6 %fusion.78 = f32[512]{0:T(512)S(1)} fusion(f32[64,8,16,128]{3,2,1,0:T(8,128)} %bitcast.64, bf16[2048,768]{1,0:T(8,128)(2,1)S(1)} %get-tuple-element.698, f32[2048]{0:T(1024)S(1)} %get-tuple-element.696, f32[512]{0:T(512)S(1)} %dynamic_slice.127, f32[512]{0:T(512)S(1)} %dynamic-slice_negate_fusion.4, s32[2048]{0:T(1024)S(1)} %fusion.77, ...), kind=kOutput, calls=%fused_computation.4.clone.1 | convolution fusion | flops 1619000832 | bytes 8151044 | tf_op jit(solution)/shard_map/while/body/eval_jaxpr/dot_general | solution.py:62
  160.2 0.6 dynamic_slice.126
  163.3 2.4 broadcast_in_dim.65
  167.2 5.6 %fusion.78 = f32[512]{0:T(512)S(1)} fusion(f32[64,8,16,128]{3,2,1,0:T(8,128)} %bitcast.64, bf16[2048,768]{1,0:T(8,128)(2,1)S(1)} %get-tuple-element.698, f32[2048]{0:T(1024)S(1)} %get-tuple-element.696, f32[512]{0:T(512)S(1)} %dynamic_slice.127, f32[512]{0:T(512)S(1)} %dynamic-slice_negate_fusion.4, s32[2048]{0:T(1024)S(1)} %fusion.77, ...), kind=kOutput, calls=%fused_computation.4.clone.1 | convolution fusion | flops 1619000832 | bytes 8151044 | tf_op jit(solution)/shard_map/while/body/eval_jaxpr/dot_general | solution.py:62
  173.0 0.6 dynamic_slice.126
  176.1 2.4 broadcast_in_dim.65
  180.0 5.6 %fusion.78 = f32[512]{0:T(512)S(1)} fusion(f32[64,8,16,128]{3,2,1,0:T(8,128)} %bitcast.64, bf16[2048,768]{1,0:T(8,128)(2,1)S(1)} %get-tuple-element.698, f32[2048]{0:T(1024)S(1)} %get-tuple-element.696, f32[512]{0:T(512)S(1)} %dynamic_slice.127, f32[512]{0:T(512)S(1)} %dynamic-slice_negate_fusion.4, s32[2048]{0:T(1024)S(1)} %fusion.77, ...), kind=kOutput, calls=%fused_computation.4.clone.1 | convolution fusion | flops 1619000832 | bytes 8151044 | tf_op jit(solution)/shard_map/while/body/eval_jaxpr/dot_general | solution.py:62
  185.7 0.6 dynamic_slice.126
  188.8 2.4 broadcast_in_dim.65
  192.7 5.6 %fusion.78 = f32[512]{0:T(512)S(1)} fusion(f32[64,8,16,128]{3,2,1,0:T(8,128)} %bitcast.64, bf16[2048,768]{1,0:T(8,128)(2,1)S(1)} %get-tuple-element.698, f32[2048]{0:T(1024)S(1)} %get-tuple-element.696, f32[512]{0:T(512)S(1)} %dynamic_slice.127, f32[512]{0:T(512)S(1)} %dynamic-slice_negate_fusion.4, s32[2048]{0:T(1024)S(1)} %fusion.77, ...), kind=kOutput, calls=%fused_computation.4.clone.1 | convolution fusion | flops 1619000832 | bytes 8151044 | tf_op jit(solution)/shard_map/while/body/eval_jaxpr/dot_general | solution.py:62
  198.4 0.6 dynamic_slice.126
  201.5 2.4 broadcast_in_dim.65
  205.4 5.6 %fusion.78 = f32[512]{0:T(512)S(1)} fusion(f32[64,8,16,128]{3,2,1,0:T(8,128)} %bitcast.64, bf16[2048,768]{1,0:T(8,128)(2,1)S(1)} %get-tuple-element.698, f32[2048]{0:T(1024)S(1)} %get-tuple-element.696, f32[512]{0:T(512)S(1)} %dynamic_slice.127, f32[512]{0:T(512)S(1)} %dynamic-slice_negate_fusion.4, s32[2048]{0:T(1024)S(1)} %fusion.77, ...), kind=kOutput, calls=%fused_computation.4.clone.1 | convolution fusion | flops 1619000832 | bytes 8151044 | tf_op jit(solution)/shard_map/while/body/eval_jaxpr/dot_general | solution.py:62
  211.1 0.6 dynamic_slice.126
  214.2 2.4 broadcast_in_dim.65
  218.1 5.6 %fusion.78 = f32[512]{0:T(512)S(1)} fusion(f32[64,8,16,128]{3,2,1,0:T(8,128)} %bitcast.64, bf16[2048,768]{1,0:T(8,128)(2,1)S(1)} %get-tuple-element.698, f32[2048]{0:T(1024)S(1)} %get-tuple-element.696, f32[512]{0:T(512)S(1)} %dynamic_slice.127, f32[512]{0:T(512)S(1)} %dynamic-slice_negate_fusion.4, s32[2048]{0:T(1024)S(1)} %fusion.77, ...), kind=kOutput, calls=%fused_computation.4.clone.1 | convolution fusion | flops 1619000832 | bytes 8151044 | tf_op jit(solution)/shard_map/while/body/eval_jaxpr/dot_general | solution.py:62
  223.8 19.6 %all-gather.1 = f32[16,1,4096]{2,1,0:T(1,128)S(1)} all-gather(f32[1,1,4096]{2,1,0:T(1,128)S(1)} %reshape.42), channel_id=1, replica_groups=mesh['row'=8,'col'=16] {'col'}, dimensions={0}, use_global_device_ids=true | all-gather | bytes 278528 | tf_op jit(solution)/shard_map/all_gather | solution.py:81
  243.7 19.4 %all-gather.3 = f32[8,1,256]{2,1,0:T(1,128)S(1)} all-gather(f32[1,1,256]{2,1,0:T(1,128)S(1)} %bitcast.71), channel_id=1, replica_groups=mesh['row'=8,'col'=16] {'row'}, dimensions={0}, use_global_device_ids=true | all-gather | bytes 9216 | tf_op jit(solution)/shard_map/all_gather | solution.py:83
  263.1 114.8 %while.27 = (s32[]{:T(128)}, f32[8,512,256]{2,1,0:T(8,128)}, s32[8]{0:T(128)S(1)}, s32[4096]{0:T(1024)S(1)}, f32[32,16]{1,0:T(8,128)S(1)}, /*index=5*/f32[4096]{...) while((s32[]{:T(128)}, f32[8,512,256]{2,1,0:T(8,128)}, ...), condition=%wide.region_7.8_spmd.clone, body=%wide.region_6.7_spmd.clone.sunk | while | flops 2162196992 | bytes 13960894 | solution.py:96
  263.1 0.6 dynamic_slice.132
  266.0 2.4 broadcast_in_dim.66
  269.9 7.6 %fusion.83 = f32[8,512,256]{2,1,0:T(8,128)} fusion(f32[8,512,256]{2,1,0:T(8,128)} %get-tuple-element.730, s32[]{:T(128)} %get-tuple-element.729, bf16[2048,256]{1,0:T(8,128)(2,1)} %get-tuple-element.764, f32[64,8,16,128]{3,2,1,0:T(8,128)} %bitcast.63, bf16[2048,768]{1,0:T(8,128)(2,1)S(1)} %get-tuple-element.760, f32[2048]{0:T(1024)S(1)} %get-tuple-element.763, ...), kind=kOutput, calls=%fused_computation.28.clone.1 | convolution fusion | flops 2162163712 | bytes 9740804 | tf_op jit(solution)/shard_map/while/body/eval_jaxpr/dot_general | solution.py:93
  280.3 2.4 broadcast_in_dim.66
  284.2 7.6 %fusion.83 = f32[8,512,256]{2,1,0:T(8,128)} fusion(f32[8,512,256]{2,1,0:T(8,128)} %get-tuple-element.730, s32[]{:T(128)} %get-tuple-element.729, bf16[2048,256]{1,0:T(8,128)(2,1)} %get-tuple-element.764, f32[64,8,16,128]{3,2,1,0:T(8,128)} %bitcast.63, bf16[2048,768]{1,0:T(8,128)(2,1)S(1)} %get-tuple-element.760, f32[2048]{0:T(1024)S(1)} %get-tuple-element.763, ...), kind=kOutput, calls=%fused_computation.28.clone.1 | convolution fusion | flops 2162163712 | bytes 9740804 | tf_op jit(solution)/shard_map/while/body/eval_jaxpr/dot_general | solution.py:93
  291.8 0.6 dynamic_slice.132
  294.7 2.4 broadcast_in_dim.66
  298.6 7.6 %fusion.83 = f32[8,512,256]{2,1,0:T(8,128)} fusion(f32[8,512,256]{2,1,0:T(8,128)} %get-tuple-element.730, s32[]{:T(128)} %get-tuple-element.729, bf16[2048,256]{1,0:T(8,128)(2,1)} %get-tuple-element.764, f32[64,8,16,128]{3,2,1,0:T(8,128)} %bitcast.63, bf16[2048,768]{1,0:T(8,128)(2,1)S(1)} %get-tuple-element.760, f32[2048]{0:T(1024)S(1)} %get-tuple-element.763, ...), kind=kOutput, calls=%fused_computation.28.clone.1 | convolution fusion | flops 2162163712 | bytes 9740804 | tf_op jit(solution)/shard_map/while/body/eval_jaxpr/dot_general | solution.py:93
  306.1 0.6 dynamic_slice.132
  309.0 2.4 broadcast_in_dim.66
  312.9 7.6 %fusion.83 = f32[8,512,256]{2,1,0:T(8,128)} fusion(f32[8,512,256]{2,1,0:T(8,128)} %get-tuple-element.730, s32[]{:T(128)} %get-tuple-element.729, bf16[2048,256]{1,0:T(8,128)(2,1)} %get-tuple-element.764, f32[64,8,16,128]{3,2,1,0:T(8,128)} %bitcast.63, bf16[2048,768]{1,0:T(8,128)(2,1)S(1)} %get-tuple-element.760, f32[2048]{0:T(1024)S(1)} %get-tuple-element.763, ...), kind=kOutput, calls=%fused_computation.28.clone.1 | convolution fusion | flops 2162163712 | bytes 9740804 | tf_op jit(solution)/shard_map/while/body/eval_jaxpr/dot_general | solution.py:93
  320.5 0.6 dynamic_slice.132
  323.4 2.4 broadcast_in_dim.66
  327.2 7.6 %fusion.83 = f32[8,512,256]{2,1,0:T(8,128)} fusion(f32[8,512,256]{2,1,0:T(8,128)} %get-tuple-element.730, s32[]{:T(128)} %get-tuple-element.729, bf16[2048,256]{1,0:T(8,128)(2,1)} %get-tuple-element.764, f32[64,8,16,128]{3,2,1,0:T(8,128)} %bitcast.63, bf16[2048,768]{1,0:T(8,128)(2,1)S(1)} %get-tuple-element.760, f32[2048]{0:T(1024)S(1)} %get-tuple-element.763, ...), kind=kOutput, calls=%fused_computation.28.clone.1 | convolution fusion | flops 2162163712 | bytes 9740804 | tf_op jit(solution)/shard_map/while/body/eval_jaxpr/dot_general | solution.py:93
  337.8 2.4 broadcast_in_dim.66
  341.6 7.7 %fusion.83 = f32[8,512,256]{2,1,0:T(8,128)} fusion(f32[8,512,256]{2,1,0:T(8,128)} %get-tuple-element.730, s32[]{:T(128)} %get-tuple-element.729, bf16[2048,256]{1,0:T(8,128)(2,1)} %get-tuple-element.764, f32[64,8,16,128]{3,2,1,0:T(8,128)} %bitcast.63, bf16[2048,768]{1,0:T(8,128)(2,1)S(1)} %get-tuple-element.760, f32[2048]{0:T(1024)S(1)} %get-tuple-element.763, ...), kind=kOutput, calls=%fused_computation.28.clone.1 | convolution fusion | flops 2162163712 | bytes 9740804 | tf_op jit(solution)/shard_map/while/body/eval_jaxpr/dot_general | solution.py:93
  349.3 0.6 dynamic_slice.132
  352.2 2.4 broadcast_in_dim.66
  356.0 7.6 %fusion.83 = f32[8,512,256]{2,1,0:T(8,128)} fusion(f32[8,512,256]{2,1,0:T(8,128)} %get-tuple-element.730, s32[]{:T(128)} %get-tuple-element.729, bf16[2048,256]{1,0:T(8,128)(2,1)} %get-tuple-element.764, f32[64,8,16,128]{3,2,1,0:T(8,128)} %bitcast.63, bf16[2048,768]{1,0:T(8,128)(2,1)S(1)} %get-tuple-element.760, f32[2048]{0:T(1024)S(1)} %get-tuple-element.763, ...), kind=kOutput, calls=%fused_computation.28.clone.1 | convolution fusion | flops 2162163712 | bytes 9740804 | tf_op jit(solution)/shard_map/while/body/eval_jaxpr/dot_general | solution.py:93
  366.5 2.4 broadcast_in_dim.66
  370.4 7.6 %fusion.83 = f32[8,512,256]{2,1,0:T(8,128)} fusion(f32[8,512,256]{2,1,0:T(8,128)} %get-tuple-element.730, s32[]{:T(128)} %get-tuple-element.729, bf16[2048,256]{1,0:T(8,128)(2,1)} %get-tuple-element.764, f32[64,8,16,128]{3,2,1,0:T(8,128)} %bitcast.63, bf16[2048,768]{1,0:T(8,128)(2,1)S(1)} %get-tuple-element.760, f32[2048]{0:T(1024)S(1)} %get-tuple-element.763, ...), kind=kOutput, calls=%fused_computation.28.clone.1 | convolution fusion | flops 2162163712 | bytes 9740804 | tf_op jit(solution)/shard_map/while/body/eval_jaxpr/dot_general | solution.py:93
  378.0 126.0 %all-reduce.2.cloned.1.call-done = f32[4096,256]{1,0:T(8,128)} async-done(((f32[4096,256]{1,0:T(8,128)}), f32[4096,256]{1,0:T(8,128)}) %all-reduce.2.cloned.1.call-update) | async-done | bytes 4194320 | tf_op jit(solution)/shard_map/psum | solution.py:97
  504.0 1.7 constant_dynamic-slice_fusion.2
  (122 shorter events, 7.6 us)
Async XLA Ops:
  6.5 68.8 %all-gather.10.cloned.1.call-start = ((), (), s32[]{:S(2)}) async-start(), calls=%async_computation.1 | async-start | bytes 3538944 | tf_op jit(solution)/shard_map/all_gather | solution.py:35
  7.3 110.6 %all-gather.8.cloned.1.call-start = ((), (), s32[]{:S(2)}) async-start(), calls=%async_computation | async-start | bytes 6684672 | tf_op jit(solution)/shard_map/all_gather | solution.py:31
  8.0 255.1 %all-gather.12.cloned.1.call-start = ((), (), s32[]{:S(2)}) async-start(), calls=%async_computation.2 | async-start | bytes 1179648 | tf_op jit(solution)/shard_map/all_gather | solution.py:37
  8.7 495.2 %all-reduce.2.cloned.1.call-start = ((), (), s32[]{:S(2)}) async-start(), calls=%async_computation.3 | async-start | bytes 8388608 | tf_op jit(solution)/shard_map/psum | solution.py:97
  75.3 46.6 %copy-start = (bf16[2048,768]{1,0:T(8,128)(2,1)S(1)}, bf16[2048,768]{1,0:T(8,128)(2,1)}, u32[]{:S(2)}) copy-start(bf16[2048,768]{1,0:T(8,128)(2,1)} %all-gather.10.cloned.1.call-done) | copy-start | bytes 9437188
Sparse Core Ops, SparseCore 0:
  9.7 65.6 all-gather.9
  77.0 40.7 all-gather.7
  120.2 45.7 all-gather.11
  378.1 125.8 all-reduce.1
